TPU v7x, 32 devices: a whole 2x2x4 slice. The times are simulated.
32 devices in a mesh: gx: 2 (over y), gy: 4 (over x, core), gz: 4 (over z).
Axes of the slice: x: 2, y: 2, z: 4, core: 2. Of those that a mesh axis runs over, the one named last changes fastest.
Arguments:
- phase_stack: float32 [512, 65536], P(None, ('gx', 'gy', 'gz')), may hold values from -40 to 40
- start_basis: float32 [512, 64], replicated, may hold values from -6 to 6
Outputs:
- corrected: float32 [512, 65536], P(None, ('gx', 'gy', 'gz'))
All inputs are finite; a program needn't handle non-finite values.
Results may differ from a plain program's by a relative error of at most 0.0003.
Values sent between devices are 32-bit elements; how exact they have to be, the bound alone decides.
A program may use at most 64 MiB of HBM per device.

v0:
```python
import functools
import itertools

import jax
import jax.numpy as jnp
from jax import lax
from jax.experimental import pallas as pl
from jax.experimental.pallas import tpu as pltpu
from jax.sharding import PartitionSpec as P

ITERS = 3
EPSILON = 1e-06
HIGHEST = lax.Precision.HIGHEST
MESH = pl.DeviceIdType.MESH
AXES = ("gx", "gy", "gz")
F32 = jnp.float32
BF16 = jnp.bfloat16
LANES = 128
STRIP = 1024


def split(value):
    high = value.astype(BF16)
    return high, (value - high.astype(F32)).astype(BF16)


def dot_nt(a, b, **kw):
    return lax.dot_general(a, b, (((1,), (1,)), ((), ())), preferred_element_type=F32, **kw)


def dot_tn(a, b, **kw):
    return lax.dot_general(a, b, (((0,), (0,)), ((), ())), preferred_element_type=F32, **kw)


def dot_nn(a, b, **kw):
    return lax.dot_general(a, b, (((1,), (0,)), ((), ())), preferred_element_type=F32, **kw)


def orthonormal_rows(rows):
    k = rows.shape[0]
    inner = dot_nt(rows, rows, precision=HIGHEST)
    eye = (
        lax.broadcasted_iota(jnp.int32, (k, k), 0) == lax.broadcasted_iota(jnp.int32, (k, k), 1)
    ).astype(F32)
    work = jnp.concatenate([eye, inner], axis=1)
    groups = [work[g : g + 8] for g in range(0, k, 8)]
    wide = (8, 2 * k)
    sub = lax.broadcasted_iota(jnp.int32, wide, 0)

    def across(value, lane):
        return jnp.broadcast_to(value[:, lane : lane + 1], wide)

    def down(value, row):
        return jnp.broadcast_to(value[row : row + 1], wide)

    def stack(entries):
        out = jnp.zeros(wide, F32)
        for row, entry in entries:
            out = jnp.where(sub == row, entry, out)
        return out

    def tree(terms):
        while len(terms) > 1:
            terms = [sum(terms[t + 1 : t + 2], terms[t]) for t in range(0, len(terms), 2)]
        return terms[0]

    finished = []
    for home in range(len(groups)):
        base = k + 8 * home
        panel = groups[home]
        columns = [across(panel, base + j) for j in range(8)]
        below = [[across(groups[g], base + j) for j in range(8)] for g in range(home + 1, k // 8)]
        e = [[down(columns[j], i) for j in range(i + 1)] for i in range(8)]
        low = [[None] * 8 for _ in range(8)]
        roots = []
        for j in range(8):
            inv = 1.0 / e[j][j]
            roots.append(lax.rsqrt(e[j][j]))
            for i in range(j + 1, 8):
                low[i][j] = e[i][j] * inv
            for i in range(j + 1, 8):
                for c in range(j + 1, i + 1):
                    e[i][c] = e[i][c] - low[i][j] * e[c][j]
        w = [[None] * 8 for _ in range(8)]
        for i in range(8):
            for j in range(i):
                terms = [low[i][j]] + [low[i][c] * w[c][j] for c in range(j + 1, i)]
                w[i][j] = -tree(terms)
        for i in range(8):
            for j in range(i):
                w[i][j] = w[i][j] * roots[i]
            w[i][i] = roots[i]
        panel = tree(
            [stack([(i, w[i][j]) for i in range(j, 8)]) * down(panel, j) for j in range(8)]
        )
        finished.append(panel)
        if below:
            back = tree(
                [stack([(j, w[i][j]) for j in range(i + 1)]) * down(panel, i) for i in range(8)]
            )
            back = [down(back, j) for j in range(8)]
            for g, cols in enumerate(below):
                at = home + 1 + g
                groups[at] = groups[at] - tree([c * r for c, r in zip(cols, back)])
    inverse = jnp.concatenate(finished, axis=0)[:, :k]
    return dot_nn(inverse, rows, precision=HIGHEST)


def pieces(m, n):
    nb = m // LANES
    blocks = [(i, j) for i in range(nb) for j in range(i, nb)]
    rows = len(blocks) * LANES // n
    out = []
    for b, (i, j) in enumerate(blocks):
        at, end = b * LANES, (b + 1) * LANES
        while at < end:
            chunk, low = divmod(at, rows)
            take = min(end - at, rows - low)
            out.append((chunk, low, i, j, at - b * LANES, take))
            at += take
    return rows, out


def pack_shape(shape):
    return 2, shape[0] * (shape[1] // 2), shape[2]


def slot(chunk, planes, columns):
    return chunk // (planes * columns), chunk // columns % planes, chunk % columns


def kernel(
    shape, x_hbm, basis_hbm, res_ref, scale_ref,
    x, basis, xh, xl, half, cross, packed, pair_in, middle, plane_in, part, column_in, total,
    gh, gl, vt, own, sums,
    x_sem, basis_sem, send_sem, pair_sem, plane_sem, column_sem, up_sem, out_sem, back_sem, sums_sem,
):
    n = shape[0] * shape[1] * shape[2]
    m, width = x.shape
    me = (lax.axis_index("gx") * shape[1] + lax.axis_index("gy")) * shape[2] + lax.axis_index("gz")
    _, planes, columns = pack_shape(shape)
    chunk_rows, plan = pieces(m, n)
    gx, gy, gz = (lax.axis_index(axis) for axis in AXES)
    side, plane = lax.rem(gy, 2), gx * (shape[1] // 2) + gy // 2
    half_gy = shape[1] // 2
    order = sorted(range(1, columns), key=lambda d: min(d, columns - d))
    strips = width // STRIP

    def strip(s):
        return pl.ds(pl.multiple_of(s * STRIP, STRIP), STRIP)

    def fetch(s):
        return pltpu.make_async_copy(x_hbm.at[:, strip(s)], x.at[:, strip(s)], x_sem.at[s])

    for s in range(strips):
        fetch(s).start()

    load_basis = pltpu.make_async_copy(basis_hbm, basis, basis_sem)
    load_basis.start()

    barrier = pltpu.get_barrier_semaphore()

    others = sorted(
        itertools.product(*map(range, shape)),
        key=lambda step: -sum(min(d, size - d) for d, size in zip(step, shape)),
    )[:-1]
    here = (gx, gy, gz)
    others = [
        tuple(lax.rem(at + d, size) if d else at for at, d, size in zip(here, step, shape))
        for step in others
    ]
    for peer in others:
        pl.semaphore_signal(barrier, inc=1, device_id=peer, device_id_type=MESH)

    half[...] = jnp.zeros_like(half)
    cross[...] = jnp.zeros_like(cross)

    @pl.loop(0, strips)
    def _(s):
        fetch(s).wait()
        high, low = split(x[:, strip(s)])
        xh[:, strip(s)] = high
        xl[:, strip(s)] = low
        cross[...] += dot_nt(high, low)
        half[: m // 2] += dot_nt(high[: m // 2], high)
        half[m // 2 :, m // 2 :] += dot_nt(high[m // 2 :], high[m // 2 :])

    half[...] += cross[...] + cross[...].T
    for chunk, low, i, j, start, take in plan:
        packed[slot(chunk, planes, columns) + (slice(low, low + take),)] = half[
            i * LANES + start : i * LANES + start + take, j * LANES : (j + 1) * LANES
        ]

    pl.semaphore_wait(barrier, n - 1)

    def send(stage, source, target, arrival, peer):
        pltpu.make_async_remote_copy(
            src_ref=source,
            dst_ref=target,
            send_sem=send_sem.at[stage],
            recv_sem=arrival,
            device_id=peer,
            device_id_type=MESH,
        ).start()

    def landed(target, arrival):
        pltpu.make_async_copy(target, target, arrival).wait()

    partner = (gx, gy + 1 - 2 * side, gz)

    def in_plane(index):
        return (index // half_gy, 2 * (index % half_gy) + side, gz)

    def other_plane(d):
        return lax.rem(plane + d, planes)

    def other_column(d):
        return lax.rem(gz + d, columns)

    for d in [*range(1, planes), 0]:
        q = other_plane(d)
        send(0, packed.at[1 - side, q], pair_in.at[q], pair_sem.at[q], partner)
    for d in [*range(1, planes), 0]:
        q = other_plane(d)
        landed(pair_in.at[q], pair_sem.at[q])
        middle[q] = packed[side, q] + pair_in[q]
        if d:
            send(1, middle.at[q], plane_in.at[plane], plane_sem.at[plane], in_plane(q))
    load_basis.wait()
    vt[...] = orthonormal_rows(basis[...])
    mine = middle[plane]
    for d in range(1, planes):
        q = other_plane(d)
        landed(plane_in.at[q], plane_sem.at[q])
        mine = mine + plane_in[q]
    part[...] = mine
    for d in reversed(order):
        c = other_column(d)
        send(2, part.at[c], column_in.at[gz], column_sem.at[gz], (gx, gy, c))
    chunk_sum = part[gz]
    for d in order:
        c = other_column(d)
        landed(column_in.at[c], column_sem.at[c])
        chunk_sum = chunk_sum + column_in[c]
    total[side, plane, gz] = chunk_sum * (1.0 / (n * width))

    ready = total.at[side, plane, gz]
    for d in reversed(order):
        send(3, ready, ready, up_sem.at[gz], (gx, gy, other_column(d)))
    for d in [0, *order]:
        c = other_column(d)
        ready = total.at[side, plane, c]
        if d:
            landed(ready, up_sem.at[c])
        for e in range(1, planes):
            send(4, ready, ready, out_sem.at[plane, c], in_plane(other_plane(e)))
        send(5, ready, ready, back_sem, partner)
    for d in [0, *order]:
        c = other_column(d)
        for e in range(1, planes):
            q = other_plane(e)
            ready = total.at[side, q, c]
            landed(ready, out_sem.at[q, c])
            send(5, ready, ready, back_sem, partner)
    landed(total.at[1 - side], back_sem)

    for chunk, low, i, j, start, take in plan:
        half[
            i * LANES + start : i * LANES + start + take, j * LANES : (j + 1) * LANES
        ] = total[slot(chunk, planes, columns) + (slice(low, low + take),)]
    for i in range(m // LANES):
        for j in range(i):
            rows, cols = pl.ds(i * LANES, LANES), pl.ds(j * LANES, LANES)
            half[rows, cols] = half[cols, rows].T
    high, low = split(half[...])
    gh[...] = high
    gl[...] = low

    def advance(_, carry):
        vh, vl = split(vt[...])
        both = dot_nn(jnp.concatenate([vh, vl], axis=0), gh[...])
        k = vh.shape[0]
        fresh = both[:k] + both[k:] + dot_nn(vh, gl[...])
        vt[...] = orthonormal_rows(fresh)
        return carry

    lax.fori_loop(0, ITERS, advance, 0, unroll=True)

    vh, vl = split(vt[...])
    k = vh.shape[0]
    tall = jnp.concatenate([vh, vl], axis=0)
    left = jnp.concatenate([vh, vh, vl], axis=0).T

    def strip_power(s, power):
        both = dot_nn(tall, xh[:, strip(s)])
        loadings = both[:k] + both[k:] + dot_nn(vh, xl[:, strip(s)])
        lh, ll = split(loadings)
        residual = x[:, strip(s)] - dot_nn(left, jnp.concatenate([lh, ll, lh], axis=0))
        res_ref[:, strip(s)] = residual
        square = residual * residual
        for c in range(0, STRIP, LANES):
            power = power + square[:, c : c + LANES]
        return power

    power = lax.fori_loop(0, strips, strip_power, jnp.zeros((m, LANES), F32), unroll=True)
    own[...] = jnp.sum(power.T, axis=0, keepdims=True)
    for peer in others:
        send(6, own, sums.at[me], sums_sem, peer)

    sums[me] = own[...]
    landed(sums.at[pl.ds(0, n - 1)], sums_sem)
    row_power = jnp.sum(sums[...], axis=0) * (1.0 / (n * width))
    scale = lax.rsqrt(row_power + EPSILON)
    scale_ref[...] = jnp.broadcast_to(scale, (LANES, m)).T
    for stage, whole in enumerate([
        packed.at[0],
        plane_in.at[pl.ds(0, planes - 1)],
        column_in.at[pl.ds(0, columns - 1)],
        column_in.at[pl.ds(0, columns - 1)],
        plane_in.at[pl.ds(0, planes - 1)],
        total.at[0],
        sums.at[pl.ds(0, n - 1)],
    ]):
        landed(whole, send_sem.at[stage])


def on_device(shape, phase_stack, start_basis):
    m, width = phase_stack.shape
    k = start_basis.shape[1]
    n = shape[0] * shape[1] * shape[2]
    assert shape[1] % 2 == 0
    chunk_rows, _ = pieces(m, n)
    sides, planes, columns = pack_shape(shape)
    chunk = (chunk_rows, LANES)
    vmem = pl.BlockSpec(memory_space=pltpu.VMEM)
    residual, scale = pl.pallas_call(
        functools.partial(kernel, shape),
        out_shape=(
            jax.ShapeDtypeStruct((m, width), F32),
            jax.ShapeDtypeStruct((m, LANES), F32),
        ),
        in_specs=[pl.BlockSpec(memory_space=pltpu.HBM)] * 2,
        out_specs=(vmem, vmem),
        scratch_shapes=[
            pltpu.VMEM((m, width), F32),
            pltpu.VMEM((k, m), F32),
            pltpu.VMEM((m, width), BF16),
            pltpu.VMEM((m, width), BF16),
            pltpu.VMEM((m, m), F32),
            pltpu.VMEM((m, m), F32),
            pltpu.VMEM((sides, planes, columns, *chunk), F32),
            pltpu.VMEM((planes, columns, *chunk), F32),
            pltpu.VMEM((planes, columns, *chunk), F32),
            pltpu.VMEM((planes, columns, *chunk), F32),
            pltpu.VMEM((columns, *chunk), F32),
            pltpu.VMEM((columns, *chunk), F32),
            pltpu.VMEM((sides, planes, columns, *chunk), F32),
            pltpu.VMEM((m, m), BF16),
            pltpu.VMEM((m, m), BF16),
            pltpu.VMEM((k, m), F32),
            pltpu.VMEM((1, m), F32),
            pltpu.VMEM((n, 1, m), F32),
            pltpu.SemaphoreType.DMA((width // STRIP,)),
            pltpu.SemaphoreType.DMA,
            pltpu.SemaphoreType.DMA((7,)),
            pltpu.SemaphoreType.DMA((planes,)),
            pltpu.SemaphoreType.DMA((planes,)),
            pltpu.SemaphoreType.DMA((columns,)),
            pltpu.SemaphoreType.DMA((columns,)),
            pltpu.SemaphoreType.DMA((planes, columns)),
            pltpu.SemaphoreType.DMA,
            pltpu.SemaphoreType.DMA,
        ],
        compiler_params=pltpu.CompilerParams(
            collective_id=0, has_side_effects=True, vmem_limit_bytes=40 << 20
        ),
        name="common_mode",
    )(
        pltpu.with_memory_space_constraint(phase_stack, pltpu.HBM),
        pltpu.with_memory_space_constraint(start_basis.T, pltpu.HBM),
    )
    return residual * scale[:, :1]


def solution(mesh):
    shape = tuple(mesh.shape[a] for a in AXES)
    return jax.shard_map(
        functools.partial(on_device, shape),
        mesh=mesh,
        in_specs=(P(None, AXES), P()),
        out_specs=P(None, AXES),
        check_vma=False,
    )
```

profile of v0, /device:TPU:0, one launch (start us, length us, event | category | flops | bytes accessed | tf_op | source)
XLA Modules:
  0.0 46.4 jit_solution(15051006515843001484)
XLA Ops:
  0.0 43.9 %common_mode.1 = (f32[512,2048]{1,0:T(8,128)S(1)}, f32[512,128]{1,0:T(8,128)S(1)}) custom-call(f32[512,2048]{1,0:T(8,128)} %x_hbm.1, f32[64,512]{1,0:T(8,128)} %bitcast.1), custom_call_target="tpu_custom_call" | custom-call | tf_op jit(solution)/shard_map/common_mode/pallas_call | solution.py:336
  43.9 0.1 slice_reduce_fusion
  44.0 2.4 %broadcast_multiply_fusion = f32[512,2048]{1,0:T(8,128)} fusion(f32[512,2048]{1,0:T(8,128)S(1)} %get-tuple-element.7, f32[512]{0:T(512)S(1)} %slice_reduce_fusion), kind=kLoop, calls=%fused_computation | loop fusion | flops 1048576 | bytes 8390656 | tf_op jit(solution)/shard_map/mul | solution.py:382
where the time goes:
time: 46.5 us; the launch traced here: 46.4 us
  Pallas kernels  43.9 us (94%)
  other arithmetic  2.36 us (5%)
    pallas_call x1, Pallas kernels, on_device(): pl.pallas_call(functools.partial(kernel, shape), out_shape=(jax.ShapeDtyp...  43.9 us
    mul x1, other arithmetic, on_device(): return residual * scale[:, :1]  2.36 us

commit v1 on v0

--- a/solution.py
+++ b/solution.py
@@ -17,6 +17,8 @@
 BF16 = jnp.bfloat16
 LANES = 128
 STRIP = 1024
+PIECES = 5
+STEPS = (4, 4)
 
 
 def split(value):
@@ -36,7 +38,7 @@
     return lax.dot_general(a, b, (((1,), (0,)), ((), ())), preferred_element_type=F32, **kw)
 
 
-def orthonormal_rows(rows):
+def orthonormal_steps(rows):
     k = rows.shape[0]
     inner = dot_nt(rows, rows, precision=HIGHEST)
     eye = (
@@ -102,8 +104,14 @@
             for g, cols in enumerate(below):
                 at = home + 1 + g
                 groups[at] = groups[at] - tree([c * r for c, r in zip(cols, back)])
+        yield None
     inverse = jnp.concatenate(finished, axis=0)[:, :k]
-    return dot_nn(inverse, rows, precision=HIGHEST)
+    yield dot_nn(inverse, rows, precision=HIGHEST)
+
+
+def orthonormal_rows(rows):
+    *_, result = orthonormal_steps(rows)
+    return result
 
 
 def pieces(m, n):
@@ -122,28 +130,32 @@
 
 
 def pack_shape(shape):
-    return 2, shape[0] * (shape[1] // 2), shape[2]
-
-
-def slot(chunk, planes, columns):
-    return chunk // (planes * columns), chunk // columns % planes, chunk % columns
+    return 2, shape[0] * (shape[1] // 2), PIECES
+
+
+def slot(chunk, dims):
+    out = []
+    for size in reversed(dims):
+        chunk, at = divmod(chunk, size)
+        out.append(at)
+    return tuple(reversed(out))
 
 
 def kernel(
     shape, x_hbm, basis_hbm, res_ref, scale_ref,
     x, basis, xh, xl, half, cross, packed, pair_in, middle, plane_in, part, column_in, total,
     gh, gl, vt, own, sums,
-    x_sem, basis_sem, send_sem, pair_sem, plane_sem, column_sem, up_sem, out_sem, back_sem, sums_sem,
+    x_sem, basis_sem, send_sem, pair_sem, plane_sem, column_sem, out_sem, back_sem, sums_sem,
 ):
     n = shape[0] * shape[1] * shape[2]
     m, width = x.shape
     me = (lax.axis_index("gx") * shape[1] + lax.axis_index("gy")) * shape[2] + lax.axis_index("gz")
-    _, planes, columns = pack_shape(shape)
-    chunk_rows, plan = pieces(m, n)
+    dims = pack_shape(shape)
+    planes, columns = dims[1], shape[2]
+    _, plan = pieces(m, dims[0] * dims[1] * dims[2])
     gx, gy, gz = (lax.axis_index(axis) for axis in AXES)
     side, plane = lax.rem(gy, 2), gx * (shape[1] // 2) + gy // 2
     half_gy = shape[1] // 2
-    order = sorted(range(1, columns), key=lambda d: min(d, columns - d))
     strips = width // STRIP
 
     def strip(s):
@@ -187,7 +199,7 @@
 
     half[...] += cross[...] + cross[...].T
     for chunk, low, i, j, start, take in plan:
-        packed[slot(chunk, planes, columns) + (slice(low, low + take),)] = half[
+        packed[slot(chunk, dims) + (slice(low, low + take),)] = half[
             i * LANES + start : i * LANES + start + take, j * LANES : (j + 1) * LANES
         ]
 
@@ -217,57 +229,67 @@
     def other_column(d):
         return lax.rem(gz + d, columns)
 
-    for d in [*range(1, planes), 0]:
-        q = other_plane(d)
-        send(0, packed.at[1 - side, q], pair_in.at[q], pair_sem.at[q], partner)
-    for d in [*range(1, planes), 0]:
-        q = other_plane(d)
-        landed(pair_in.at[q], pair_sem.at[q])
-        middle[q] = packed[side, q] + pair_in[q]
-        if d:
-            send(1, middle.at[q], plane_in.at[plane], plane_sem.at[plane], in_plane(q))
+    away_first = [*range(1, planes), 0]
+    basis_steps = []
+
+    def work(steps=1):
+        for _ in range(steps):
+            for step in basis_steps:
+                step = next(step, None)
+                if step is not None:
+                    vt[...] = step
+
+    for p in range(PIECES):
+        for d in away_first:
+            q = other_plane(d)
+            send(0, packed.at[1 - side, q, p], pair_in.at[q, p], pair_sem.at[q, p], partner)
     load_basis.wait()
-    vt[...] = orthonormal_rows(basis[...])
-    mine = middle[plane]
-    for d in range(1, planes):
-        q = other_plane(d)
-        landed(plane_in.at[q], plane_sem.at[q])
-        mine = mine + plane_in[q]
-    part[...] = mine
-    for d in reversed(order):
-        c = other_column(d)
-        send(2, part.at[c], column_in.at[gz], column_sem.at[gz], (gx, gy, c))
-    chunk_sum = part[gz]
-    for d in order:
-        c = other_column(d)
-        landed(column_in.at[c], column_sem.at[c])
-        chunk_sum = chunk_sum + column_in[c]
-    total[side, plane, gz] = chunk_sum * (1.0 / (n * width))
-
-    ready = total.at[side, plane, gz]
-    for d in reversed(order):
-        send(3, ready, ready, up_sem.at[gz], (gx, gy, other_column(d)))
-    for d in [0, *order]:
-        c = other_column(d)
-        ready = total.at[side, plane, c]
-        if d:
-            landed(ready, up_sem.at[c])
-        for e in range(1, planes):
-            send(4, ready, ready, out_sem.at[plane, c], in_plane(other_plane(e)))
-        send(5, ready, ready, back_sem, partner)
-    for d in [0, *order]:
-        c = other_column(d)
-        for e in range(1, planes):
-            q = other_plane(e)
-            ready = total.at[side, q, c]
-            landed(ready, out_sem.at[q, c])
-            send(5, ready, ready, back_sem, partner)
+    for p in range(PIECES):
+        for d in away_first:
+            q = other_plane(d)
+            landed(pair_in.at[q, p], pair_sem.at[q, p])
+            middle[q, p] = packed[side, q, p] + pair_in[q, p]
+            if d:
+                send(1, middle.at[q, p], plane_in.at[plane, p], plane_sem.at[plane, p], in_plane(q))
+    basis_steps.append(orthonormal_steps(basis[...]))
+    work(STEPS[0])
+    for p in range(PIECES):
+        value = middle[plane, p]
+        for d in range(1, planes):
+            q = other_plane(d)
+            landed(plane_in.at[q, p], plane_sem.at[q, p])
+            value = value + plane_in[q, p]
+        part[p] = value
+        for d in range(1, columns):
+            c = other_column(d)
+            send(2, part.at[p], column_in.at[gz, p], column_sem.at[gz, p], (gx, gy, c))
+        column_in[gz, p] = value
+    work(STEPS[1])
+    for p in range(PIECES):
+        for d in range(1, columns):
+            c = other_column(d)
+            landed(column_in.at[c, p], column_sem.at[c, p])
+        value = column_in[0, p]
+        for c in range(1, columns):
+            value = value + column_in[c, p]
+        total[side, plane, p] = value * (1.0 / (n * width))
+        ready = total.at[side, plane, p]
+        for d in range(1, planes):
+            send(3, ready, ready, out_sem.at[plane, p], in_plane(other_plane(d)))
+        send(4, ready, ready, back_sem, partner)
+    work(99)
+    for p in range(PIECES):
+        for d in range(1, planes):
+            q = other_plane(d)
+            ready = total.at[side, q, p]
+            landed(ready, out_sem.at[q, p])
+            send(4, ready, ready, back_sem, partner)
     landed(total.at[1 - side], back_sem)
 
     for chunk, low, i, j, start, take in plan:
         half[
             i * LANES + start : i * LANES + start + take, j * LANES : (j + 1) * LANES
-        ] = total[slot(chunk, planes, columns) + (slice(low, low + take),)]
+        ] = total[slot(chunk, dims) + (slice(low, low + take),)]
     for i in range(m // LANES):
         for j in range(i):
             rows, cols = pl.ds(i * LANES, LANES), pl.ds(j * LANES, LANES)
@@ -305,7 +327,7 @@
     power = lax.fori_loop(0, strips, strip_power, jnp.zeros((m, LANES), F32), unroll=True)
     own[...] = jnp.sum(power.T, axis=0, keepdims=True)
     for peer in others:
-        send(6, own, sums.at[me], sums_sem, peer)
+        send(5, own, sums.at[me], sums_sem, peer)
 
     sums[me] = own[...]
     landed(sums.at[pl.ds(0, n - 1)], sums_sem)
@@ -313,11 +335,10 @@
     scale = lax.rsqrt(row_power + EPSILON)
     scale_ref[...] = jnp.broadcast_to(scale, (LANES, m)).T
     for stage, whole in enumerate([
-        packed.at[0],
-        plane_in.at[pl.ds(0, planes - 1)],
+        total.at[0],
+        total.at[0, pl.ds(0, planes - 1)],
         column_in.at[pl.ds(0, columns - 1)],
-        column_in.at[pl.ds(0, columns - 1)],
-        plane_in.at[pl.ds(0, planes - 1)],
+        total.at[0, pl.ds(0, planes - 1)],
         total.at[0],
         sums.at[pl.ds(0, n - 1)],
     ]):
@@ -329,9 +350,10 @@
     k = start_basis.shape[1]
     n = shape[0] * shape[1] * shape[2]
     assert shape[1] % 2 == 0
-    chunk_rows, _ = pieces(m, n)
-    sides, planes, columns = pack_shape(shape)
-    chunk = (chunk_rows, LANES)
+    sides, planes, _ = pack_shape(shape)
+    columns = shape[2]
+    chunk_rows, _ = pieces(m, sides * planes * PIECES)
+    chunk = (PIECES, chunk_rows, LANES)
     vmem = pl.BlockSpec(memory_space=pltpu.VMEM)
     residual, scale = pl.pallas_call(
         functools.partial(kernel, shape),
@@ -348,13 +370,13 @@
             pltpu.VMEM((m, width), BF16),
             pltpu.VMEM((m, m), F32),
             pltpu.VMEM((m, m), F32),
-            pltpu.VMEM((sides, planes, columns, *chunk), F32),
-            pltpu.VMEM((planes, columns, *chunk), F32),
-            pltpu.VMEM((planes, columns, *chunk), F32),
-            pltpu.VMEM((planes, columns, *chunk), F32),
+            pltpu.VMEM((sides, planes, *chunk), F32),
+            pltpu.VMEM((planes, *chunk), F32),
+            pltpu.VMEM((planes, *chunk), F32),
+            pltpu.VMEM((planes, *chunk), F32),
+            pltpu.VMEM(chunk, F32),
             pltpu.VMEM((columns, *chunk), F32),
-            pltpu.VMEM((columns, *chunk), F32),
-            pltpu.VMEM((sides, planes, columns, *chunk), F32),
+            pltpu.VMEM((sides, planes, *chunk), F32),
             pltpu.VMEM((m, m), BF16),
             pltpu.VMEM((m, m), BF16),
             pltpu.VMEM((k, m), F32),
@@ -362,12 +384,11 @@
             pltpu.VMEM((n, 1, m), F32),
             pltpu.SemaphoreType.DMA((width // STRIP,)),
             pltpu.SemaphoreType.DMA,
-            pltpu.SemaphoreType.DMA((7,)),
-            pltpu.SemaphoreType.DMA((planes,)),
-            pltpu.SemaphoreType.DMA((planes,)),
-            pltpu.SemaphoreType.DMA((columns,)),
-            pltpu.SemaphoreType.DMA((columns,)),
-            pltpu.SemaphoreType.DMA((planes, columns)),
+            pltpu.SemaphoreType.DMA((6,)),
+            pltpu.SemaphoreType.DMA((planes, PIECES)),
+            pltpu.SemaphoreType.DMA((planes, PIECES)),
+            pltpu.SemaphoreType.DMA((columns, PIECES)),
+            pltpu.SemaphoreType.DMA((planes, PIECES)),
             pltpu.SemaphoreType.DMA,
             pltpu.SemaphoreType.DMA,
         ],

time: 46.5 us -> 43.8 us (0.942)
  Pallas kernels: 43.9 us -> 41.2 us
    pallas_call x1, Pallas kernels: 43.9 us -> 41.2 us  [on_device(): pl.pallas_call(functools.partial(kernel, shape), out_shape=(jax.ShapeDtyp...]
where the time goes in v1:
time: 43.8 us; the launch traced here: 43.7 us
  Pallas kernels  41.2 us (94%)
  other arithmetic  2.36 us (5%)
    pallas_call x1, Pallas kernels, on_device(): pl.pallas_call(functools.partial(kernel, shape), out_shape=(jax.ShapeDtyp...  41.2 us
    mul x1, other arithmetic, on_device(): return residual * scale[:, :1]  2.36 us

profile of v1, /device:TPU:0, one launch (start us, length us, event | category | flops | bytes accessed | tf_op | source)
XLA Modules:
  0.0 43.7 jit_solution(18406498796503149893)
XLA Ops:
  0.0 41.2 %common_mode.1 = (f32[512,2048]{1,0:T(8,128)S(1)}, f32[512,128]{1,0:T(8,128)S(1)}) custom-call(f32[512,2048]{1,0:T(8,128)} %x_hbm.1, f32[64,512]{1,0:T(8,128)} %bitcast.1), custom_call_target="tpu_custom_call" | custom-call | tf_op jit(solution)/shard_map/common_mode/pallas_call | solution.py:358
  41.2 0.1 slice_reduce_fusion
  41.3 2.4 %broadcast_multiply_fusion = f32[512,2048]{1,0:T(8,128)} fusion(f32[512,2048]{1,0:T(8,128)S(1)} %get-tuple-element.7, f32[512]{0:T(512)S(1)} %slice_reduce_fusion), kind=kLoop, calls=%fused_computation | loop fusion | flops 1048576 | bytes 8390656 | tf_op jit(solution)/shard_map/mul | solution.py:403
